TPU v7x, 32 devices: a whole 2x2x4 slice. The times are simulated.
32 devices in a mesh: cuts: 4 (over x, core), fiber: 8 (over z, y).
Axes of the slice: x: 2, y: 2, z: 4, core: 2. Of those that a mesh axis runs over, the one named last changes fastest.
Arguments:
- tile_vals: bfloat16 [131072, 128], P(('cuts', 'fiber')), may hold values from -6 to 6
- tile_count: int32 [131072], P(('cuts', 'fiber')), may hold values from 1 to 128
- tile_dest: int32 [131072, 1], P(('cuts', 'fiber')), may hold values from 0 to 3; in each aligned block of 4096 rows (0 to 4095, 4096 to 8191, ...) at most 2048 rows name the same one
- tile_row: int32 [131072], P(('cuts', 'fiber')), may hold values from 0 to 1023, as said below
- tile_block: int32 [131072], P(('cuts', 'fiber')), may hold values from 0 to 3
- tile_first: int32 [131072], P(('cuts', 'fiber')), may hold values from 0 to 255
- factor_one: bfloat16 [8192, 32], P(('cuts', 'fiber')), may hold values from -1.5 to 1.5
- factor_three: bfloat16 [4096, 32], P('fiber'), may hold values from -0.5 to 0.5
- factor_two: bfloat16 [4096, 32], P(('cuts', 'fiber')), may hold values from -0.09375 to 0.09375
Outputs:
- ttmc: bfloat16 [4096, 1024], P(('cuts', 'fiber'))
- projected: float32 [4096, 32], P(('cuts', 'fiber'))
Inputs may be any that keep to these rules, and one draw needn't show every extreme that they name: `tile_dest`: among the tiles of one device, each index of cuts is named at most 2048 times, and exactly 2048 times by some. `tile_row`: among the tiles of one device, each block of 128 consecutive values (starting at multiples of 128) is taken exactly 512 times.
All inputs are finite; a program needn't handle non-finite values.
Results may differ from a plain program's by a relative error of at most 0.002.
Values may be sent and summed in bfloat16 or wider, within the bound.
A program may use at most 128 MiB of HBM per device.

v0:
```python
import jax
import jax.numpy as jnp
from jax import lax
from jax.sharding import PartitionSpec as P

R1 = 32
R3 = 32
FIBER = 128
I2_DEV = 1024


def project_tiles(values, block_ids, factor_three):
    blocks = factor_three.shape[0] // FIBER
    table = factor_three.reshape(blocks, FIBER, R3).transpose(1, 0, 2).reshape(FIBER, blocks * R3)
    every = jnp.dot(values, table, preferred_element_type=jnp.float32).reshape(
        values.shape[0], blocks, R3
    )
    pick = (block_ids[:, None] == jnp.arange(blocks, dtype=jnp.int32)[None, :]).astype(jnp.float32)
    return jnp.sum(every * pick[:, :, None], axis=1)


def slot_of(owners, owner_count, capacity):
    member = (owners[:, None] == jnp.arange(owner_count, dtype=jnp.int32)[None, :]).astype(
        jnp.int32
    )
    before = jnp.cumsum(member, axis=0) - member
    return owners * capacity + jnp.sum(before * member, axis=1)


def place_into(values, slot_ids, owner_count, capacity):
    buffer = jnp.zeros((owner_count * capacity,) + values.shape[1:], values.dtype)
    return buffer.at[slot_ids].set(values).reshape((owner_count, capacity) + values.shape[1:])


def body(
    tile_vals,
    tile_count,
    tile_dest,
    tile_row,
    tile_block,
    tile_first,
    factor_one,
    factor_three,
    factor_two,
):
    ncuts = lax.axis_size("cuts")
    tiles = tile_vals.shape[0]
    positions = jnp.arange(FIBER, dtype=jnp.int32)
    masked = jnp.where(
        positions[None, :] < tile_count[:, None], tile_vals, jnp.zeros_like(tile_vals)
    )
    dest = tile_dest[:, 0]
    first_rows = jnp.take(factor_one, tile_first, axis=0)
    fiber_count = lax.axis_size("fiber")
    block_rows = I2_DEV // fiber_count
    fiber_cap = tiles // fiber_count
    fiber_slots = fiber_count * fiber_cap
    row_owner = tile_row // block_rows
    fiber_slot = slot_of(row_owner, fiber_count, fiber_cap)
    local_proj = project_tiles(masked, tile_block, factor_three)
    first_wide = first_rows.astype(jnp.float32)
    combined = dest * block_rows + tile_row % block_rows
    got_proj, got_first, got_rows = (
        lax.all_to_all(
            place_into(local_proj, fiber_slot, fiber_count, fiber_cap),
            "fiber",
            split_axis=0,
            concat_axis=0,
            tiled=True,
        ),
        lax.all_to_all(
            place_into(first_wide, fiber_slot, fiber_count, fiber_cap),
            "fiber",
            split_axis=0,
            concat_axis=0,
            tiled=True,
        ),
        lax.all_to_all(
            place_into(combined[:, None], fiber_slot, fiber_count, fiber_cap),
            "fiber",
            split_axis=0,
            concat_axis=0,
            tiled=True,
        ),
    )
    proj = got_proj.reshape(fiber_slots, R3)
    first_f = got_first.reshape(fiber_slots, R1)
    target = got_rows.reshape(fiber_slots)
    kron = (first_f[:, :, None] * proj[:, None, :]).reshape(fiber_slots, R1 * R3)
    partial_rows = jax.ops.segment_sum(kron, target, num_segments=ncuts * block_rows)
    summed = lax.psum_scatter(partial_rows, "cuts", scatter_dimension=0, tiled=True)
    ttmc = summed.astype(jnp.bfloat16)
    local_gram = lax.dot_general(
        ttmc, factor_two, (((0,), (0,)), ((), ())), preferred_element_type=jnp.float32
    )
    gram = lax.psum(local_gram, ("cuts", "fiber"))
    gram_b = gram.astype(jnp.bfloat16)
    projected = jnp.dot(ttmc, gram_b, preferred_element_type=jnp.float32) / 32.0
    return (ttmc, projected)


def solution(mesh):
    in_specs = (
        P(("cuts", "fiber"), None),
        P(("cuts", "fiber")),
        P(("cuts", "fiber"), None),
        P(("cuts", "fiber")),
        P(("cuts", "fiber")),
        P(("cuts", "fiber")),
        P(("cuts", "fiber"), None),
        P("fiber", None),
        P(("cuts", "fiber"), None),
    )
    out_specs = (P(("cuts", "fiber"), None), P(("cuts", "fiber"), None))
    return jax.shard_map(body, mesh=mesh, in_specs=in_specs, out_specs=out_specs, check_vma=False)
```

profile of v0, /device:TPU:0, one launch (start us, length us, event | category | flops | bytes accessed | tf_op | source)
XLA Modules:
  0.0 238.0 jit_solution(2505887969231628959)
XLA Ops:
  7.2 0.0 copy-start
  7.2 0.7 broadcast_multiply_fusion.1
  7.9 0.8 reshape.76
  8.7 0.7 fusion.21
  9.4 0.7 fusion.24
  10.2 2.3 reduce-window.6
  12.5 0.3 slice_reduce_fusion
  12.8 0.2 reduce-window.9
  13.0 0.1 add_bitcast_fusion
  13.1 0.1 fusion.18
  13.2 2.2 fusion.3
  15.5 0.0 copy-start.2
  15.5 2.0 copy.31
  17.4 0.0 copy-done.2
  17.5 11.4 %scatter_custom_fusion.2 = f32[4096,32]{1,0:T(8,128)S(1)} fusion(s32[4096]{0:T(1024)S(1)} %get-tuple-element.4, f32[4096,32]{1,0:T(8,128)} %copy.31, f32[]{:T(128)} %constant.50.clone.1), kind=kCustom, calls=%fused_computation.16 | custom fusion | bytes 524800 | tf_op jit(solution)/shard_map/scatter | solution.py:32
  28.9 0.0 copy-start.3
  28.9 1.4 copy.32
  30.3 7.3 %all-to-all-start.2 = ((f32[8,512,32]{1,2,0:T(8,128)}), f32[8,512,32]{1,2,0:T(8,128)S(1)}, u32[]{:S(2)}, u32[]{:S(2)}) async-start(f32[8,512,32]{1,2,0:T(8,128)} %copy.32), calls=%async_computation.2 | async-start | bytes 1048576 | tf_op jit(solution)/shard_map/all_to_all | solution.py:64
  37.6 0.0 copy-done.3
  37.6 0.1 copy.27
  37.7 25.8 %scatter_custom_fusion.1 = f32[4096,32]{1,0:T(8,128)S(1)} fusion(s32[4096]{0:T(1024)S(1)} %get-tuple-element.4, f32[]{:T(128)} %constant.50.clone.1, pred[4096]{0:T(1024)(128)(4,1)S(1)} %compare_and_fusion, bf16[]{:T(256)} %constant.61.clone.1, bf16[256,32]{1,0:T(8,128)(2,1)S(1)} %copy.27, s32[4096]{0:T(1024)S(1)} %get-tuple-element.5), kind=kCustom, calls=%fused_computation.8 | custom fusion | flops 262144 | bytes 610310 | tf_op jit(solution)/shard_map/scatter | solution.py:32
  63.5 1.4 copy.28
  64.9 0.0 all-to-all-done.2
  64.9 6.0 %all-to-all-start.1 = ((f32[8,512,32]{1,2,0:T(8,128)}), f32[8,512,32]{1,2,0:T(8,128)S(1)}, u32[]{:S(2)}, u32[]{:S(2)}) async-start(f32[8,512,32]{1,2,0:T(8,128)} %copy.28), calls=%async_computation.1 | async-start | bytes 1048576 | tf_op jit(solution)/shard_map/all_to_all | solution.py:71
  70.9 16.1 %scatter_custom_fusion = s32[4096]{0:T(1024)} fusion(s32[4096]{0:T(1024)S(1)} %get-tuple-element.4, s32[4096]{0:T(1024)S(1)} %get-tuple-element.2, s32[]{:T(128)} %constant.51.clone.1), kind=kCustom, calls=%fused_computation.51 | custom fusion | bytes 16388 | tf_op jit(solution)/shard_map/scatter | solution.py:32
  87.0 0.0 all-to-all-done.1
  87.0 6.0 %all-to-all-start = ((s32[8,512,1]{1,2,0:T(1,128)}), s32[8,512,1]{1,2,0:T(1,128)S(1)}, u32[]{:S(2)}, u32[]{:S(2)}) async-start(s32[8,512,1]{1,2,0:T(1,128)} %bitcast.3), calls=%async_computation | async-start | bytes 32768 | tf_op jit(solution)/shard_map/all_to_all | solution.py:78
  93.0 0.2 reduce-scatter.2.cloned.1.call-start
  93.3 7.8 %broadcast_multiply_fusion = f32[4096,32,32]{0,2,1:T(8,128)} fusion(f32[4096,32]{0,1:T(8,128)S(1)} %bitcast.53, f32[4096,32]{0,1:T(8,128)S(1)} %bitcast.54), kind=kLoop, calls=%fused_computation.5 | loop fusion | flops 4194304 | bytes 17825792 | tf_op jit(solution)/shard_map/mul | solution.py:89
  101.1 17.5 %copy.34 = f32[4096,1024]{1,0:T(8,128)} copy(f32[4096,1024]{0,1:T(8,128)} %bitcast.50) | data formatting | bytes 33554432 | tf_op jit(solution)/shard_map/mul | solution.py:89
  118.6 0.0 all-to-all-done
  118.6 37.7 %scatter_custom_fusion.3 = f32[512,1024]{1,0:T(8,128)} fusion(s32[4096]{0:T(1024)S(1)} %bitcast.61, f32[4096,1024]{1,0:T(8,128)} %copy.34, f32[]{:T(128)} %constant.50.clone.1), kind=kCustom, calls=%fused_computation.19 | custom fusion | flops 4194304 | bytes 2097664 | tf_op jit(solution)/shard_map/scatter-add | solution.py:90
  156.3 0.0 reduce-scatter.2.cloned.1.call-update
  156.3 32.5 %reduce-scatter.2.cloned.1.call-done = f32[128,1024]{1,0:T(8,128)} async-done(((f32[512,1024]{1,0:T(8,128)}), f32[128,1024]{1,0:T(8,128)}) %reduce-scatter.2.cloned.1.call-update) | async-done | bytes 524304 | tf_op jit(solution)/shard_map/reduce_scatter | solution.py:91
  188.9 1.1 convert_element_type.27
  189.9 0.0 copy-done
  190.0 0.0 copy-start.1
  190.0 0.2 fusion.32
  190.1 40.2 %all-reduce.1 = bf16[1024,32]{0,1:T(8,128)(2,1)S(1)} all-reduce(f32[1024,32]{0,1:T(8,128)S(1)} %fusion.32), channel_id=1, replica_groups=mesh['cuts'=4,'fiber'=8] {'cuts','fiber'}, use_global_device_ids=true, to_apply=%region_9.10 | all-reduce | flops 32768 | bytes 196608 | tf_op jit(solution)/shard_map/psum | solution.py:96
  230.4 0.8 convolution_multiply_fusion.1
  231.2 0.0 copy-done.1
  (5 shorter events, 0.1 us)
Async XLA Ops:
  7.2 182.8 %copy-start = (bf16[128,32]{0,1:T(8,128)(2,1)S(1)}, bf16[128,32]{0,1:T(8,128)(2,1)}, u32[]{:S(2)}) copy-start(bf16[128,32]{0,1:T(8,128)(2,1)} %param.17) | copy-start | bytes 24580
  15.5 2.0 copy-start.2
  28.9 8.7 %copy-start.3 = (bf16[256,32]{0,1:T(8,128)(2,1)S(1)}, bf16[256,32]{0,1:T(8,128)(2,1)}, u32[]{:S(2)}) copy-start(bf16[256,32]{0,1:T(8,128)(2,1)} %param.15) | copy-start | bytes 49156
  30.3 34.6 %all-to-all-start.2 = ((f32[8,512,32]{1,2,0:T(8,128)}), f32[8,512,32]{1,2,0:T(8,128)S(1)}, u32[]{:S(2)}, u32[]{:S(2)}) async-start(f32[8,512,32]{1,2,0:T(8,128)} %copy.32), calls=%async_computation.2 | async-start | bytes 1048576 | tf_op jit(solution)/shard_map/all_to_all | solution.py:64
  64.9 22.1 %all-to-all-start.1 = ((f32[8,512,32]{1,2,0:T(8,128)}), f32[8,512,32]{1,2,0:T(8,128)S(1)}, u32[]{:S(2)}, u32[]{:S(2)}) async-start(f32[8,512,32]{1,2,0:T(8,128)} %copy.28), calls=%async_computation.1 | async-start | bytes 1048576 | tf_op jit(solution)/shard_map/all_to_all | solution.py:71
  87.0 31.5 %all-to-all-start = ((s32[8,512,1]{1,2,0:T(1,128)}), s32[8,512,1]{1,2,0:T(1,128)S(1)}, u32[]{:S(2)}, u32[]{:S(2)}) async-start(s32[8,512,1]{1,2,0:T(1,128)} %bitcast.3), calls=%async_computation | async-start | bytes 32768 | tf_op jit(solution)/shard_map/all_to_all | solution.py:78
  93.0 95.8 %reduce-scatter.2.cloned.1.call-start = ((), (), s32[]{:S(2)}) async-start(), calls=%async_computation.4 | async-start | bytes 2621440 | tf_op jit(solution)/shard_map/reduce_scatter | solution.py:91
  190.0 41.2 %copy-start.1 = (bf16[128,1024]{1,0:T(8,128)(2,1)}, bf16[128,1024]{1,0:T(8,128)(2,1)S(1)}, u32[]{:S(2)}) copy-start(bf16[128,1024]{1,0:T(8,128)(2,1)S(1)} %convert_element_type.27) | copy-start | bytes 786436
Sparse Core Ops, SparseCore 0:
  156.4 32.3 reduce-scatter.1
where the time goes:
time: 239 us; the launch traced here: 238 us
  other arithmetic  77.3 us (32%)
  local copies, waits for them, and re-layouts  51 us (21%)
  blocking collectives  40.2 us (17%)
  waiting for transfers between devices  32.6 us (14%)
  starting transfers between devices  19.5 us (8%)
  between operations  14.2 us (6%)
  matrix products  3.18 us (1%)
    psum x1, blocking collectives, body(): gram = lax.psum(local_gram, ('cuts', 'fiber'))  40.2 us
    scatter-add x1, other arithmetic, body(): jax.ops.segment_sum(kron, target, num_segments=ncuts * block_rows)  37.7 us
    reduce_scatter x1, waiting for transfers between devices, body(): lax.psum_scatter(partial_rows, 'cuts', scatter_dimension=0, tiled=True)  32.5 us
    scatter x2, local copies, waits for them, and re-layouts, place_into(): buffer.at[slot_ids].set(values)  27.5 us
    scatter x1, other arithmetic, place_into(): buffer.at[slot_ids].set(values)  25.8 us
    mul x3, local copies, waits for them, and re-layouts, body(): first_f[:, :, None] * proj[:, None, :]  17.5 us
    mul x1, other arithmetic, body(): first_f[:, :, None] * proj[:, None, :]  7.8 us
    all_to_all x1, starting transfers between devices, body(): lax.all_to_all(place_into(local_proj, fiber_slot, fiber_count, fiber_cap)...  7.31 us
  transfers between devices with their start and end apart: 4, of which 1 were waited for; matrix products, arithmetic and copies ran while one was open for 29% of the time, Pallas kernels for 0%

commit v1 on v0

--- a/solution.py
+++ b/solution.py
@@ -93,7 +93,8 @@
     local_gram = lax.dot_general(
         ttmc, factor_two, (((0,), (0,)), ((), ())), preferred_element_type=jnp.float32
     )
-    gram = lax.psum(local_gram, ("cuts", "fiber"))
+    pieces = lax.all_gather(local_gram, ("cuts", "fiber"))
+    gram = jnp.sum(pieces, axis=0)
     gram_b = gram.astype(jnp.bfloat16)
     projected = jnp.dot(ttmc, gram_b, preferred_element_type=jnp.float32) / 32.0
     return (ttmc, projected)

time: 239 us -> 268 us (1.12)
  waiting for transfers between devices: 32.6 us -> 96.1 us
  blocking collectives: 40.2 us -> 0 us
  local copies, waits for them, and re-layouts: 51 us -> 55.6 us
    all_gather x0 -> x1, waiting for transfers between devices: none -> 63.6 us  [body(): pieces = lax.all_gather(local_gram, ('cuts', 'fiber'))]
    psum x1 -> x0, blocking collectives: 40.2 us -> none  [body(): gram = lax.psum(local_gram, ('cuts', 'fiber'))]
    unnamed x9 -> x10, local copies, waits for them, and re-layouts: 0.15 us -> 4.76 us
  transfers between devices with their start and end apart: 4 -> 5, of which waited for: 1 -> 2; matrix products, arithmetic and copies ran while one was open for 29% -> 26% of each run, Pallas kernels for 0% -> 0%
where the time goes in v1:
time: 268 us; the launch traced here: 267 us
  waiting for transfers between devices  96.1 us (36%)
  other arithmetic  78 us (29%)
  local copies, waits for them, and re-layouts  55.6 us (21%)
  starting transfers between devices  19.6 us (7%)
  between operations  14.2 us (5%)
  matrix products  3.84 us (1%)
    all_gather x1, waiting for transfers between devices, body(): pieces = lax.all_gather(local_gram, ('cuts', 'fiber'))  63.6 us
    scatter-add x1, other arithmetic, body(): jax.ops.segment_sum(kron, target, num_segments=ncuts * block_rows)  37.7 us
    reduce_scatter x1, waiting for transfers between devices, body(): lax.psum_scatter(partial_rows, 'cuts', scatter_dimension=0, tiled=True)  32.5 us
    scatter x2, local copies, waits for them, and re-layouts, place_into(): buffer.at[slot_ids].set(values)  27.5 us
    scatter x1, other arithmetic, place_into(): buffer.at[slot_ids].set(values)  25.8 us
    mul x3, local copies, waits for them, and re-layouts, body(): first_f[:, :, None] * proj[:, None, :]  17.5 us
    mul x1, other arithmetic, body(): first_f[:, :, None] * proj[:, None, :]  7.8 us
    all_to_all x1, starting transfers between devices, body(): lax.all_to_all(place_into(local_proj, fiber_slot, fiber_count, fiber_cap)...  7.31 us
  transfers between devices with their start and end apart: 5, of which 2 were waited for; matrix products, arithmetic and copies ran while one was open for 26% of the time, Pallas kernels for 0%

profile of v1, /device:TPU:0, one launch (start us, length us, event | category | flops | bytes accessed | tf_op | source)
XLA Modules:
  0.0 267.3 jit_solution(3690859597496152133)
XLA Ops:
  7.2 0.0 copy-start
  7.2 0.7 broadcast_multiply_fusion.1
  7.9 0.8 reshape.76
  8.7 0.7 fusion.21
  9.4 0.7 fusion.24
  10.2 2.3 reduce-window.6
  12.5 0.3 slice_reduce_fusion
  12.8 0.2 reduce-window.9
  13.0 0.1 add_bitcast_fusion
  13.1 0.1 fusion.18
  13.2 2.2 fusion.3
  15.5 0.0 copy-start.2
  15.5 2.0 copy.31
  17.4 0.0 copy-done.2
  17.5 11.4 %scatter_custom_fusion.2 = f32[4096,32]{1,0:T(8,128)S(1)} fusion(s32[4096]{0:T(1024)S(1)} %get-tuple-element.4, f32[4096,32]{1,0:T(8,128)} %copy.31, f32[]{:T(128)} %constant.50.clone.1), kind=kCustom, calls=%fused_computation.17 | custom fusion | bytes 524800 | tf_op jit(solution)/shard_map/scatter | solution.py:32
  28.9 0.0 copy-start.3
  28.9 1.4 copy.32
  30.3 7.3 %all-to-all-start.2 = ((f32[8,512,32]{1,2,0:T(8,128)}), f32[8,512,32]{1,2,0:T(8,128)S(1)}, u32[]{:S(2)}, u32[]{:S(2)}) async-start(f32[8,512,32]{1,2,0:T(8,128)} %copy.32), calls=%async_computation.2 | async-start | bytes 1048576 | tf_op jit(solution)/shard_map/all_to_all | solution.py:64
  37.6 0.0 copy-done.3
  37.6 0.1 copy.27
  37.7 25.8 %scatter_custom_fusion.1 = f32[4096,32]{1,0:T(8,128)S(1)} fusion(s32[4096]{0:T(1024)S(1)} %get-tuple-element.4, f32[]{:T(128)} %constant.50.clone.1, pred[4096]{0:T(1024)(128)(4,1)S(1)} %compare_and_fusion, bf16[]{:T(256)} %constant.61.clone.1, bf16[256,32]{1,0:T(8,128)(2,1)S(1)} %copy.27, s32[4096]{0:T(1024)S(1)} %get-tuple-element.5), kind=kCustom, calls=%fused_computation.9 | custom fusion | flops 262144 | bytes 610310 | tf_op jit(solution)/shard_map/scatter | solution.py:32
  63.5 1.4 copy.28
  64.9 0.0 all-to-all-done.2
  64.9 6.0 %all-to-all-start.1 = ((f32[8,512,32]{1,2,0:T(8,128)}), f32[8,512,32]{1,2,0:T(8,128)S(1)}, u32[]{:S(2)}, u32[]{:S(2)}) async-start(f32[8,512,32]{1,2,0:T(8,128)} %copy.28), calls=%async_computation.1 | async-start | bytes 1048576 | tf_op jit(solution)/shard_map/all_to_all | solution.py:71
  70.9 16.1 %scatter_custom_fusion = s32[4096]{0:T(1024)} fusion(s32[4096]{0:T(1024)S(1)} %get-tuple-element.4, s32[4096]{0:T(1024)S(1)} %get-tuple-element.2, s32[]{:T(128)} %constant.51.clone.1), kind=kCustom, calls=%fused_computation.52 | custom fusion | bytes 16388 | tf_op jit(solution)/shard_map/scatter | solution.py:32
  87.0 0.0 all-to-all-done.1
  87.0 6.0 %all-to-all-start = ((s32[8,512,1]{1,2,0:T(1,128)}), s32[8,512,1]{1,2,0:T(1,128)S(1)}, u32[]{:S(2)}, u32[]{:S(2)}) async-start(s32[8,512,1]{1,2,0:T(1,128)} %bitcast.3), calls=%async_computation | async-start | bytes 32768 | tf_op jit(solution)/shard_map/all_to_all | solution.py:78
  93.0 0.2 reduce-scatter.2.cloned.1.call-start
  93.3 7.8 %broadcast_multiply_fusion = f32[4096,32,32]{0,2,1:T(8,128)} fusion(f32[4096,32]{0,1:T(8,128)S(1)} %bitcast.59, f32[4096,32]{0,1:T(8,128)S(1)} %bitcast.60), kind=kLoop, calls=%fused_computation.5 | loop fusion | flops 4194304 | bytes 17825792 | tf_op jit(solution)/shard_map/mul | solution.py:89
  101.1 17.5 %copy.34 = f32[4096,1024]{1,0:T(8,128)} copy(f32[4096,1024]{0,1:T(8,128)} %bitcast.55) | data formatting | bytes 33554432 | tf_op jit(solution)/shard_map/mul | solution.py:89
  118.6 0.0 all-to-all-done
  118.6 37.7 %scatter_custom_fusion.3 = f32[512,1024]{1,0:T(8,128)} fusion(s32[4096]{0:T(1024)S(1)} %bitcast.67, f32[4096,1024]{1,0:T(8,128)} %copy.34, f32[]{:T(128)} %constant.50.clone.1), kind=kCustom, calls=%fused_computation.20 | custom fusion | flops 4194304 | bytes 2097664 | tf_op jit(solution)/shard_map/scatter-add | solution.py:90
  156.3 0.0 reduce-scatter.2.cloned.1.call-update
  156.3 0.0 all-gather.3.cloned.1.call-start
  156.4 32.5 %reduce-scatter.2.cloned.1.call-done = f32[128,1024]{1,0:T(8,128)} async-done(((f32[512,1024]{1,0:T(8,128)}), f32[128,1024]{1,0:T(8,128)}) %reduce-scatter.2.cloned.1.call-update) | async-done | bytes 524304 | tf_op jit(solution)/shard_map/reduce_scatter | solution.py:91
  188.9 1.1 convert_element_type.27
  189.9 0.0 copy-done
  190.0 0.0 copy-start.1
  190.0 0.8 fusion.32
  190.8 0.0 all-gather.3.cloned.1.call-update
  190.8 63.6 %all-gather.3.cloned.1.call-done = f32[32768,32]{0,1:T(8,128)} async-done(((f32[1024,32]{0,1:T(8,128)}), f32[32768,32]{0,1:T(8,128)}) %all-gather.3.cloned.1.call-update) | async-done | bytes 4194320 | tf_op jit(solution)/shard_map/all_gather | solution.py:96
  254.4 4.6 %copy.38 = f32[4,8,32,1024]{3,2,1,0:T(8,128)S(1)} copy(f32[4,8,32,1024]{3,1,2,0:T(8,128)} %bitcast.58) | data formatting | bytes 8388608
  259.0 0.6 bitcast_reduce_fusion
  259.6 0.0 copy-done.1
  259.6 0.8 convolution_multiply_fusion.1
  (5 shorter events, 0.1 us)
Async XLA Ops:
  7.2 182.8 %copy-start = (bf16[128,32]{0,1:T(8,128)(2,1)S(1)}, bf16[128,32]{0,1:T(8,128)(2,1)}, u32[]{:S(2)}) copy-start(bf16[128,32]{0,1:T(8,128)(2,1)} %param.17) | copy-start | bytes 24580
  15.5 2.0 copy-start.2
  28.9 8.7 %copy-start.3 = (bf16[256,32]{0,1:T(8,128)(2,1)S(1)}, bf16[256,32]{0,1:T(8,128)(2,1)}, u32[]{:S(2)}) copy-start(bf16[256,32]{0,1:T(8,128)(2,1)} %param.15) | copy-start | bytes 49156
  30.3 34.6 %all-to-all-start.2 = ((f32[8,512,32]{1,2,0:T(8,128)}), f32[8,512,32]{1,2,0:T(8,128)S(1)}, u32[]{:S(2)}, u32[]{:S(2)}) async-start(f32[8,512,32]{1,2,0:T(8,128)} %copy.32), calls=%async_computation.2 | async-start | bytes 1048576 | tf_op jit(solution)/shard_map/all_to_all | solution.py:64
  64.9 22.1 %all-to-all-start.1 = ((f32[8,512,32]{1,2,0:T(8,128)}), f32[8,512,32]{1,2,0:T(8,128)S(1)}, u32[]{:S(2)}, u32[]{:S(2)}) async-start(f32[8,512,32]{1,2,0:T(8,128)} %copy.28), calls=%async_computation.1 | async-start | bytes 1048576 | tf_op jit(solution)/shard_map/all_to_all | solution.py:71
  87.0 31.5 %all-to-all-start = ((s32[8,512,1]{1,2,0:T(1,128)}), s32[8,512,1]{1,2,0:T(1,128)S(1)}, u32[]{:S(2)}, u32[]{:S(2)}) async-start(s32[8,512,1]{1,2,0:T(1,128)} %bitcast.3), calls=%async_computation | async-start | bytes 32768 | tf_op jit(solution)/shard_map/all_to_all | solution.py:78
  93.0 95.8 %reduce-scatter.2.cloned.1.call-start = ((), (), s32[]{:S(2)}) async-start(), calls=%async_computation.4 | async-start | bytes 2621440 | tf_op jit(solution)/shard_map/reduce_scatter | solution.py:91
  156.3 98.0 %all-gather.3.cloned.1.call-start = ((), (), s32[]{:S(2)}) async-start(), calls=%async_computation.5 | async-start | bytes 4325376 | tf_op jit(solution)/shard_map/all_gather | solution.py:96
  190.0 69.7 %copy-start.1 = (bf16[128,1024]{1,0:T(8,128)(2,1)}, bf16[128,1024]{1,0:T(8,128)(2,1)S(1)}, u32[]{:S(2)}) copy-start(bf16[128,1024]{1,0:T(8,128)(2,1)S(1)} %convert_element_type.27) | copy-start | bytes 786436
Sparse Core Ops, SparseCore 0:
  156.4 32.3 reduce-scatter.1
  191.9 62.4 all-gather.2
